TPU v7x, 32 devices: a whole 2x2x4 slice. The times are simulated.
32 devices in a mesh: row: 4 (over x, core), col: 8 (over z, y).
Axes of the slice: x: 2, y: 2, z: 4, core: 2. Of those that a mesh axis runs over, the one named last changes fastest.
Arguments:
- adj_trailing: bfloat16 [4096, 8192], P('row', 'col'), may hold values from -6 to 6
- panel_rows0: bfloat16 [4096, 512], P('row'), may hold values from -0.09375 to 0.09375
- panel_rows1: bfloat16 [4096, 512], P('row'), may hold values from -0.09375 to 0.09375
- panel_cols0: bfloat16 [8192, 512], P('col'), may hold values from -0.0625 to 0.0625
- panel_cols1: bfloat16 [8192, 512], P('col'), may hold values from -0.0625 to 0.0625
- inv_diag0: float32 [512, 512], replicated, as said below
- inv_diag1: float32 [512, 512], replicated, as said below
- cross_block: float32 [512, 512], replicated, may hold values from -0.25 to 0.25
- panel_adj0: bfloat16 [4096, 512], P(('row', 'col')), may hold values from -6 to 6
- panel_adj1: bfloat16 [4096, 512], P(('row', 'col')), may hold values from -6 to 6
Outputs:
- row_adj1: float32 [4096, 512], P(('row', 'col'))
- row_adj0: float32 [4096, 512], P(('row', 'col'))
- col_adj1: float32 [8192, 512], P('col')
- col_adj0: float32 [8192, 512], P('col')
- diag_adj1: float32 [512, 512], replicated
- diag_adj0: float32 [512, 512], replicated
Inputs may be any that keep to these rules, and one draw needn't show every extreme that they name: `inv_diag0`: lower triangular, with diagonal entries of 1 to 2. `inv_diag1`: lower triangular, with diagonal entries of 1 to 2.
All inputs are finite; a program needn't handle non-finite values.
Results may differ from a plain program's by a relative error of at most 0.0003.
Values sent between devices are 32-bit elements; how exact they have to be, the bound alone decides.
No kernel may reach another device: no remote copies, remote signals or barrier semaphores. Data moves between devices by JAX's collectives and lax.ppermute only.
A program may use at most 128 MiB of HBM per device.

v0:
```python
import jax
import jax.numpy as jnp
from jax import lax
from jax.sharding import PartitionSpec as P


def trailing_term(adj_trailing, columns):
    return jnp.dot(adj_trailing, columns, preferred_element_type=jnp.float32)


def column_term(adj_trailing, rows):
    return -jnp.einsum("rc,rb->cb", adj_trailing, rows, preferred_element_type=jnp.float32)


def local(
    adj_trailing,
    panel_rows0,
    panel_rows1,
    panel_cols0,
    panel_cols1,
    inv_diag0,
    inv_diag1,
    cross_block,
    panel_adj0,
    panel_adj1,
):
    highest = lax.Precision.HIGHEST
    share = panel_adj1.shape[0]
    width = panel_cols1.shape[1]
    offset = lax.axis_index("col") * share
    own_rows1 = lax.dynamic_slice_in_dim(panel_rows1, offset, share, 0).astype(jnp.float32)
    own_rows0 = lax.dynamic_slice_in_dim(panel_rows0, offset, share, 0).astype(jnp.float32)
    both_cols = jnp.concatenate((panel_cols1, panel_cols0), axis=1)
    trail = lax.psum_scatter(
        trailing_term(adj_trailing, both_cols), "col", scatter_dimension=0, tiled=True
    )
    trail1 = trail[:, :width]
    trail0 = trail[:, width:]
    both_rows = jnp.concatenate((panel_rows1, panel_rows0), axis=1)
    column_sum = lax.psum(column_term(adj_trailing, both_rows), "row")
    col_adj1 = column_sum[:, :width]
    col_adj0 = column_sum[:, width:]
    bar1 = panel_adj1.astype(jnp.float32) - trail1
    row_adj1 = jnp.dot(bar1, inv_diag1, precision=highest)
    bar0 = (
        panel_adj0.astype(jnp.float32) - trail0 - jnp.dot(row_adj1, cross_block, precision=highest)
    )
    row_adj0 = jnp.dot(bar0, inv_diag0, precision=highest)
    gram1 = jnp.dot(bar1.T, own_rows1, precision=highest)
    gram0 = jnp.dot(bar0.T, own_rows0, precision=highest)
    local1 = jnp.dot(inv_diag1.T, gram1, precision=highest)
    local0 = jnp.dot(inv_diag0.T, gram0, precision=highest)
    summed1, summed0 = lax.psum((local1, local0), ("row", "col"))
    diag_adj1 = -jnp.tril(summed1)
    diag_adj0 = -jnp.tril(summed0)
    return (row_adj1, row_adj0, col_adj1, col_adj0, diag_adj1, diag_adj0)


def solution(mesh):
    return jax.shard_map(
        local,
        mesh=mesh,
        in_specs=(
            P("row", "col"),
            P("row", None),
            P("row", None),
            P("col", None),
            P("col", None),
            P(),
            P(),
            P(),
            P(("row", "col"), None),
            P(("row", "col"), None),
        ),
        out_specs=(
            P(("row", "col"), None),
            P(("row", "col"), None),
            P("col", None),
            P("col", None),
            P(),
            P(),
        ),
        check_vma=False,
    )
```

profile of v0, /device:TPU:0, one launch (start us, length us, event | category | flops | bytes accessed | tf_op | source)
XLA Modules:
  0.0 268.3 jit_solution(9926880069097998248)
XLA Ops:
  8.0 0.0 copy-start
  8.0 0.0 reduce-scatter.2.cloned.1.call-start
  8.1 1.5 copy-done
  9.6 5.9 %convolution_bitcast_fusion = f32[1024,1024]{0,1:T(8,128)} fusion(bf16[1024,1024]{1,0:T(8,128)(2,1)S(1)} %copy-done, bf16[1024,512]{1,0:T(8,128)(2,1)} %param.13, bf16[1024,512]{1,0:T(8,128)(2,1)} %param.14), kind=kOutput, calls=%fused_computation.1 | convolution fusion | flops 2151677952 | bytes 8388608 | tf_op jit(solution)/shard_map/dot_general | solution.py:8
  15.5 0.0 copy-start.9
  15.5 0.0 reduce-scatter.2.cloned.1.call-update
  15.5 0.0 all-reduce.4.cloned.1.call-start
  15.6 1.1 copy-done.9
  16.7 5.6 %negate_bitcast_fusion = f32[1024,1024]{0,1:T(8,128)} fusion(bf16[1024,1024]{1,0:T(8,128)(2,1)S(1)} %copy-done, bf16[1024,512]{1,0:T(8,128)(2,1)} %param.11, bf16[1024,512]{1,0:T(8,128)(2,1)S(1)} %copy-done.9), kind=kOutput, calls=%fused_computation | convolution fusion | flops 2152726528 | bytes 8388608 | tf_op jit(solution)/shard_map/rc,rb->cb/dot_general | solution.py:12
  22.3 0.0 copy-start.7
  22.3 0.0 copy-start.8
  22.3 0.0 copy-start.2
  22.3 0.0 all-reduce.4.cloned.1.call-update
  22.3 0.2 all-reduce.6.cloned.1.call-start
  22.5 0.6 copy-done.7
  23.2 0.1 copy.16
  23.3 0.0 copy-done.8
  23.3 0.8 copy.17
  24.1 83.0 %reduce-scatter.2.cloned.1.call-done = f32[128,1024]{0,1:T(8,128)} async-done(((f32[1024,1024]{0,1:T(8,128)}), f32[128,1024]{0,1:T(8,128)}) %reduce-scatter.2.cloned.1.call-update) | async-done | bytes 524304 | tf_op jit(solution)/shard_map/reduce_scatter | solution.py:34
  107.1 0.0 copy-done.2
  107.1 0.0 copy-start.6
  107.1 1.8 fusion.7
  108.9 0.0 copy-done.6
  108.9 0.0 copy-start.5
  108.9 0.0 copy-start.4
  108.9 0.0 copy-start.3
  108.9 2.9 %convolution_subtract_fusion = f32[128,512]{0,1:T(8,128)S(1)} fusion(f32[128,512]{1,0:T(8,128)S(1)} %fusion.7, f32[512,512]{1,0:T(8,128)S(1)} %copy-done.6, f32[128,1024]{0,1:T(8,128)} %reduce-scatter.2.cloned.1.call-done, bf16[128,512]{0,1:T(8,128)(2,1)} %copy.17), kind=kOutput, calls=%fused_computation.10 | convolution fusion | flops 402849792 | bytes 1966080 | tf_op jit(solution)/shard_map/dot_general | solution.py:46
  111.8 0.0 copy-done.5
  111.8 1.5 fusion.8
  113.3 0.0 copy-done.4
  113.3 0.0 copy-start.1
  113.3 1.6 fusion.6
  114.9 0.0 copy-done.3
  114.9 2.8 %convolution_bitcast_fusion.2 = f32[512,512]{0,1:T(8,128)} fusion(f32[512,512]{1,0:T(8,128)S(1)} %fusion.6, f32[512,512]{1,0:T(8,128)S(1)} %copy-done.3), kind=kOutput, calls=%fused_computation.9 | convolution fusion | flops 1610612736 | bytes 3145728 | tf_op jit(solution)/shard_map/dot_general | solution.py:51
  117.8 0.0 copy-done.1
  117.8 2.8 %convolution_bitcast_fusion.1 = f32[512,512]{0,1:T(8,128)} fusion(f32[512,512]{1,0:T(8,128)S(1)} %fusion.8, f32[512,512]{1,0:T(8,128)S(1)} %copy-done.1), kind=kOutput, calls=%fused_computation.8 | convolution fusion | flops 1610612736 | bytes 3145728 | tf_op jit(solution)/shard_map/dot_general | solution.py:52
  120.6 0.0 all-reduce.6.cloned.1.call-update
  120.6 0.0 all-reduce.4.cloned.1.call-done
  120.6 4.8 %fusion.15 = (f32[1024,512]{0,1:T(8,128)}, f32[1024,512]{0,1:T(8,128)}) fusion(f32[1024,1024]{0,1:T(8,128)} %all-reduce.4.cloned.1.call-done), kind=kLoop, calls=%fused_computation.25 | loop fusion | bytes 8388608 | tf_op jit(solution)/shard_map/slice | solution.py:42
  125.5 2.9 %copy.19 = f32[1024,512]{1,0:T(8,128)} copy(f32[1024,512]{0,1:T(8,128)} %get-tuple-element.15) | data formatting | bytes 4194304
  128.4 2.9 %copy.20 = f32[1024,512]{1,0:T(8,128)} copy(f32[1024,512]{0,1:T(8,128)} %get-tuple-element.14) | data formatting | bytes 4194304
  131.3 1.5 fusion.16
  132.7 121.5 %all-reduce.6.cloned.1.call-done = (f32[512,512]{0,1:T(8,128)}, f32[512,512]{0,1:T(8,128)}) async-done(((f32[512,512]{0,1:T(8,128)}, f32[512,512]{0,1:T(8,128)}), (f32[512,512]{0,1:T(8,128)}, f32[512,512]{0,1:T(8,128)})) %all-reduce.6.cloned.1.call-update) | async-done | bytes 2097168 | tf_op jit(solution)/shard_map/psum | solution.py:53
  254.2 2.8 %select_negate_fusion = (f32[512,512]{0,1:T(8,128)S(1)}, f32[512,512]{0,1:T(8,128)}) fusion(f32[512,512]{0,1:T(8,128)} %get-tuple-element.13, f32[512,512]{0,1:T(8,128)} %get-tuple-element.12), kind=kLoop, calls=%fused_computation.11 | loop fusion | flops 1310720 | bytes 4194304 | tf_op jit(solution)/shard_map/neg | solution.py:55
  257.0 2.5 copy.21
  259.6 1.3 copy.22
Async XLA Ops:
  8.0 1.6 copy-start
  8.0 99.0 %reduce-scatter.2.cloned.1.call-start = ((), (), s32[]{:S(2)}) async-start(), calls=%async_computation.1 | async-start | bytes 4718592 | tf_op jit(solution)/shard_map/reduce_scatter | solution.py:34
  15.5 1.2 copy-start.9
  15.5 105.1 %all-reduce.4.cloned.1.call-start = ((), (), s32[]{:S(2)}) async-start(), calls=%async_computation.2 | async-start | bytes 8388608 | tf_op jit(solution)/shard_map/psum | solution.py:40
  22.3 0.9 copy-start.7
  22.3 1.0 copy-start.8
  22.3 84.8 %copy-start.2 = (f32[512,512]{1,0:T(8,128)S(1)}, f32[512,512]{1,0:T(8,128)}, u32[]{:S(2)}) copy-start(f32[512,512]{1,0:T(8,128)} %param.16) | copy-start | bytes 3145732
  22.3 231.9 %all-reduce.6.cloned.1.call-start = ((), (), s32[]{:S(2)}) async-start(), calls=%async_computation.3 | async-start | bytes 4194304 | tf_op jit(solution)/shard_map/psum | solution.py:53
  107.1 1.8 copy-start.6
  108.9 3.0 %copy-start.5 = (f32[128,512]{1,0:T(8,128)}, f32[128,512]{1,0:T(8,128)S(1)}, u32[]{:S(2)}) copy-start(f32[128,512]{1,0:T(8,128)S(1)} %fusion.7) | copy-start | bytes 786436
  108.9 4.4 %copy-start.4 = (f32[128,1024]{0,1:T(8,128)S(1)}, f32[128,1024]{0,1:T(8,128)}, u32[]{:S(2)}) copy-start(f32[128,1024]{0,1:T(8,128)} %reduce-scatter.2.cloned.1.call-done) | copy-start | bytes 1572868
  108.9 6.0 %copy-start.3 = (f32[512,512]{1,0:T(8,128)S(1)}, f32[512,512]{1,0:T(8,128)}, u32[]{:S(2)}) copy-start(f32[512,512]{1,0:T(8,128)} %param.16) | copy-start | bytes 3145732
  113.3 4.4 %copy-start.1 = (f32[512,512]{1,0:T(8,128)S(1)}, f32[512,512]{1,0:T(8,128)}, u32[]{:S(2)}) copy-start(f32[512,512]{1,0:T(8,128)} %param.15) | copy-start | bytes 3145732
Sparse Core Ops, SparseCore 0:
  15.6 91.3 reduce-scatter.1
Sparse Core Ops, SparseCore 1:
  22.4 88.0 all-reduce.3
  120.7 133.5 all-reduce.5
where the time goes:
time: 269 us; the launch traced here: 268 us
  waiting for transfers between devices  205 us (76%)
  matrix products  26.3 us (10%)
  local copies, waits for them, and re-layouts  18.7 us (7%)
  between operations  15.6 us (6%)
  other arithmetic  2.78 us (1%)
    psum x1, waiting for transfers between devices, local(): summed1, summed0 = lax.psum((local1, local0), ('row', 'col'))  122 us
    reduce_scatter x1, waiting for transfers between devices, local(): lax.psum_scatter(trailing_term(adj_trailing, both_cols), 'col', scatter_d...  83 us
    unnamed x26, local copies, waits for them, and re-layouts  13.9 us
    dot_general x1, matrix products, trailing_term(): return jnp.dot(adj_trailing, columns, preferred_element_type=jnp.float32)  5.88 us
    dot_general x1, matrix products, column_term(): jnp.einsum('rc,rb->cb', adj_trailing, rows, preferred_element_type=jnp.fl...  5.57 us
  transfers between devices with their start and end apart: 3, of which 2 were waited for; matrix products, arithmetic and copies ran while one was open for 12% of the time, Pallas kernels for 0%

commit v1 on v0

--- a/solution.py
+++ b/solution.py
@@ -50,7 +50,13 @@
     gram0 = jnp.dot(bar0.T, own_rows0, precision=highest)
     local1 = jnp.dot(inv_diag1.T, gram1, precision=highest)
     local0 = jnp.dot(inv_diag0.T, gram0, precision=highest)
-    summed1, summed0 = lax.psum((local1, local0), ("row", "col"))
+
+    def scenes_choose(u_in, row_axis, along_axis):
+        for m in (row_axis, along_axis):
+            u_in = lax.psum(u_in, m)
+        return u_in
+
+    summed1, summed0 = scenes_choose((local1, local0), "col", "row")
     diag_adj1 = -jnp.tril(summed1)
     diag_adj0 = -jnp.tril(summed0)
     return (row_adj1, row_adj0, col_adj1, col_adj0, diag_adj1, diag_adj0)

time: 269 us -> 365 us (1.36)
  waiting for transfers between devices: 205 us -> 306 us
    psum x1, waiting for transfers between devices: 0.03 us -> 120 us  [local(): column_sum = lax.psum(column_term(adj_trailing, both_rows), 'row')]
    psum x1, waiting for transfers between devices: 122 us -> 96 us  [scenes_choose(): u_in = lax.psum(u_in, m)]
    reduce_scatter x1, waiting for transfers between devices: 83 us -> 89.5 us  [local(): lax.psum_scatter(trailing_term(adj_trailing, both_cols), 'col', scatter_d...]
    unnamed x26 -> x20, local copies, waits for them, and re-layouts: 13.9 us -> 13.1 us
  transfers between devices with their start and end apart: 3 -> 3, of which waited for: 2 -> 3; matrix products, arithmetic and copies ran while one was open for 12% -> 2% of each run, Pallas kernels for 0% -> 0%
where the time goes in v1:
time: 365 us
  waiting for transfers between devices  306 us (84%)
  matrix products  24.5 us (7%)
  local copies, waits for them, and re-layouts  18 us (5%)
  between operations  13.9 us (4%)
    psum x1, waiting for transfers between devices, local(): column_sum = lax.psum(column_term(adj_trailing, both_rows), 'row')  120 us
    psum x1, waiting for transfers between devices, scenes_choose(): u_in = lax.psum(u_in, m)  96 us
    reduce_scatter x1, waiting for transfers between devices, local(): lax.psum_scatter(trailing_term(adj_trailing, both_cols), 'col', scatter_d...  89.5 us
    unnamed x20, local copies, waits for them, and re-layouts  13.1 us
  transfers between devices with their start and end apart: 3, of which 3 were waited for; matrix products, arithmetic and copies ran while one was open for 2% of the time, Pallas kernels for 0%

profile of v1, /device:TPU:0, one launch (start us, length us, event | category | flops | bytes accessed | tf_op | source)
XLA Modules:
  0.0 365.0 jit_solution(15254806995191913442)
XLA Ops:
  7.2 0.0 copy-start
  7.2 0.0 reduce-scatter.2.cloned.1.call-start
  7.2 1.5 copy-done
  8.8 5.9 %convolution_bitcast_fusion = f32[1024,1024]{0,1:T(8,128)} fusion(bf16[1024,1024]{1,0:T(8,128)(2,1)S(1)} %copy-done, bf16[1024,512]{1,0:T(8,128)(2,1)} %param.13, bf16[1024,512]{1,0:T(8,128)(2,1)} %param.14), kind=kOutput, calls=%fused_computation.1 | convolution fusion | flops 2151677952 | bytes 8388608 | tf_op jit(solution)/shard_map/dot_general | solution.py:8
  14.6 0.0 copy-start.6
  14.6 0.0 reduce-scatter.2.cloned.1.call-update
  14.7 0.0 copy-start.2
  14.7 0.0 all-reduce.5.cloned.1.call-start
  14.7 0.8 copy-done.6
  15.5 0.1 copy.16
  15.7 1.0 copy.17
  16.7 89.5 %reduce-scatter.2.cloned.1.call-done = f32[128,1024]{0,1:T(8,128)} async-done(((f32[1024,1024]{0,1:T(8,128)}), f32[128,1024]{0,1:T(8,128)}) %reduce-scatter.2.cloned.1.call-update) | async-done | bytes 524304 | tf_op jit(solution)/shard_map/reduce_scatter | solution.py:34
  106.2 0.0 copy-start.3
  106.2 1.6 fusion.6
  107.8 0.0 copy-done.2
  107.8 0.0 copy-start.5
  107.9 2.8 convolution_bitcast_fusion.2
  110.7 0.0 copy-done.3
  110.7 0.8 fusion.7
  111.5 0.0 copy-done.5
  111.5 0.0 copy-start.4
  111.5 0.0 copy-start.1
  111.5 1.8 convolution_subtract_fusion
  113.3 0.0 copy-done.4
  113.3 1.5 fusion.8
  114.8 0.0 copy-done.1
  114.8 2.8 convolution_bitcast_fusion.1
  117.6 0.0 all-reduce.5.cloned.1.call-update
  117.7 0.2 all-reduce.7.cloned.1.call-start
  117.9 5.9 %negate_bitcast_fusion = f32[1024,1024]{0,1:T(8,128)} fusion(bf16[1024,1024]{1,0:T(8,128)(2,1)S(1)} %copy-done, bf16[1024,512]{1,0:T(8,128)(2,1)} %param.11, bf16[1024,512]{1,0:T(8,128)(2,1)} %param.12), kind=kOutput, calls=%fused_computation | convolution fusion | flops 2152726528 | bytes 8388608 | tf_op jit(solution)/shard_map/rc,rb->cb/dot_general | solution.py:12
  123.8 96.0 %all-reduce.5.cloned.1.call-done = (f32[512,512]{0,1:T(8,128)}, f32[512,512]{0,1:T(8,128)}) async-done(((f32[512,512]{0,1:T(8,128)}, f32[512,512]{0,1:T(8,128)}), (f32[512,512]{0,1:T(8,128)}, f32[512,512]{0,1:T(8,128)})) %all-reduce.5.cloned.1.call-update) | async-done | bytes 2097168 | tf_op jit(solution)/shard_map/psum | solution.py:56
  219.8 0.0 all-reduce.7.cloned.1.call-update
  219.8 1.5 fusion.16
  221.3 120.0 %all-reduce.7.cloned.1.call-done = (f32[1024,1024]{0,1:T(8,128)}, f32[512,512]{0,1:T(8,128)}, f32[512,512]{0,1:T(8,128)}) async-done(((f32[1024,1024]{0,1:T(8,128)}, f32[512,512]{0,1:T(8,128)}, f32[512,512]{0,1:T(8,128)}), (f32[1024,1024]{0,1:T(8,128)}, f32[512,512]{0,1:T(8,128)}, f32[512,512]{0,1:T(8,128)})) %all-reduce.7.cloned.1.call-update) | async-done | bytes 6291472 | tf_op jit(solution)/shard_map/psum | solution.py:40
  341.2 4.8 %fusion.15 = (f32[1024,512]{0,1:T(8,128)}, f32[1024,512]{0,1:T(8,128)}) fusion(f32[1024,1024]{0,1:T(8,128)} %get-tuple-element.14), kind=kLoop, calls=%fused_computation.25 | loop fusion | bytes 8388608 | tf_op jit(solution)/shard_map/slice | solution.py:42
  346.1 2.9 copy.20
  348.9 2.9 copy.19
  351.8 2.8 select_negate_fusion
  354.6 2.5 copy.22
  357.1 1.3 copy.21
Async XLA Ops:
  7.2 1.6 copy-start
  7.2 99.1 %reduce-scatter.2.cloned.1.call-start = ((), (), s32[]{:S(2)}) async-start(), calls=%async_computation.1 | async-start | bytes 4718592 | tf_op jit(solution)/shard_map/reduce_scatter | solution.py:34
  14.6 0.9 copy-start.6
  14.7 93.2 %copy-start.2 = (f32[512,512]{1,0:T(8,128)S(1)}, f32[512,512]{1,0:T(8,128)}, u32[]{:S(2)}) copy-start(f32[512,512]{1,0:T(8,128)} %param.16) | copy-start | bytes 3145732
  14.7 205.1 %all-reduce.5.cloned.1.call-start = ((), (), s32[]{:S(2)}) async-start(), calls=%async_computation.2 | async-start | bytes 4194304 | tf_op jit(solution)/shard_map/psum | solution.py:56
  106.2 4.5 %copy-start.3 = (f32[128,1024]{0,1:T(8,128)S(1)}, f32[128,1024]{0,1:T(8,128)}, u32[]{:S(2)}) copy-start(f32[128,1024]{0,1:T(8,128)} %reduce-scatter.2.cloned.1.call-done) | copy-start | bytes 1572868
  107.8 3.6 copy-start.5
  111.5 1.8 copy-start.4
  111.5 3.3 copy-start.1
  117.7 223.6 %all-reduce.7.cloned.1.call-start = ((), (), s32[]{:S(2)}) async-start(), calls=%async_computation.3 | async-start | bytes 12582912 | tf_op jit(solution)/shard_map/psum | solution.py:40
Sparse Core Ops, SparseCore 0:
  14.8 91.4 reduce-scatter.1
  117.8 101.9 all-reduce.4
  222.3 118.8 all-reduce.6
